TPU v7x, 256 devices: a whole 4x4x8 slice. The times are simulated.
256 devices in a mesh: gx: 16 (over z_lo, x), gy: 2 (over core), gz: 8 (over z_hi, y).
Axes of the slice: x: 4, y: 4, z: 8 (z_hi: 2, z_lo: 4; z = z_hi * 4 + z_lo), core: 2. Of those that a mesh axis runs over, the one named last changes fastest.
Arguments:
- tokens: bfloat16 [128, 32, 128, 192], P('gx', 'gy', 'gz'), may hold values from -6 to 6
- upstream: bfloat16 [128, 32, 128, 192], P('gx', 'gy', 'gz'), may hold values from -6 to 6
- norm_gain: float32 [192], replicated, may hold values from 0.25 to 1.75
- norm_bias: float32 [192], replicated, may hold values from -3 to 3
- qkv_weight: bfloat16 [192, 576], replicated, may hold values from -4 to 4, as said below
- qkv_bias: float32 [576], replicated, may hold values from -3 to 3
- proj_weight: bfloat16 [192, 192], replicated, may hold values from -0.4375 to 0.4375
Outputs:
- token_grad: bfloat16 [128, 32, 128, 192], P('gx', 'gy', 'gz')
- qkv_weight_grad: float32 [192, 576], replicated
- qkv_bias_grad: float32 [576], replicated
- proj_weight_grad: float32 [192, 192], replicated
- proj_bias_grad: float32 [192], replicated
- gain_grad: float32 [192], replicated
- norm_bias_grad: float32 [192], replicated
Inputs may be any that keep to these rules, and one draw needn't show every extreme that they name: `qkv_weight`: columns are the query, key and value projections in that order, each 6 heads of 32 columns.
All inputs are finite; a program needn't handle non-finite values.
Results may differ from a plain program's by a relative error of at most 0.02.
The roundings to bfloat16 on the way count: a program that leaves them out, or rounds other values in their place, can miss the bound.
Values may be sent and summed in bfloat16 or wider, within the bound.
No kernel may reach another device: no remote copies, remote signals or barrier semaphores. Data moves between devices by JAX's collectives and lax.ppermute only.
A program may use at most 64 MiB of HBM per device.

v0:
```python
import jax
import jax.numpy as jnp
from jax import lax
from jax.sharding import PartitionSpec as P

HEADS = 6
WIN = 8
SHIFT = 4


def passed_along(value, axis, steps):
    count = lax.axis_size(axis)
    pairs = [(source, (source + steps) % count) for source in range(count)]
    return lax.ppermute(value, axis, pairs)


def window_grads(tok, upward, idents, norm_gain, norm_bias, qkv_weight, qkv_bias, proj_weight):
    length = tok.shape[0]
    width = tok.shape[1]
    heads = HEADS
    head_size = width // heads
    single = jnp.float32
    factor = head_size ** (-0.5)
    inputs = tok.astype(single)
    centred = inputs - jnp.mean(inputs, axis=-1, keepdims=True)
    inverse = lax.rsqrt(jnp.mean(centred * centred, axis=-1, keepdims=True) + 1e-05)
    normed = centred * inverse
    hidden = (normed * norm_gain + norm_bias).astype(jnp.bfloat16)
    packed = (jnp.dot(hidden, qkv_weight, preferred_element_type=single) + qkv_bias).astype(
        jnp.bfloat16
    )
    query = packed[:, :width].reshape(length, heads, head_size)
    keyset = packed[:, width : 2 * width].reshape(length, heads, head_size)
    valset = packed[:, 2 * width :].reshape(length, heads, head_size)
    scores = jnp.einsum("qhd,khd->hqk", query, keyset, preferred_element_type=single) * factor
    same = idents[:, None] == idents[None, :]
    scores = jnp.where(same[None], scores, -1e30)
    peak = jnp.max(scores, axis=-1, keepdims=True)
    expo = jnp.exp(scores - peak)
    probs = expo / jnp.sum(expo, axis=-1, keepdims=True)
    probs_half = probs.astype(jnp.bfloat16)
    attended = jnp.einsum("hqk,khd->qhd", probs_half, valset, preferred_element_type=single)
    attended = attended.reshape(length, width).astype(jnp.bfloat16)
    grad_proj = jnp.einsum("lc,lf->cf", attended, upward, preferred_element_type=single)
    grad_pbias = jnp.sum(upward.astype(single), axis=0)
    attended_grad = jnp.einsum(
        "lf,cf->lc", upward, proj_weight, preferred_element_type=single
    ).astype(jnp.bfloat16)
    attended_grad = attended_grad.reshape(length, heads, head_size)
    prob_grad = jnp.einsum("qhd,khd->hqk", attended_grad, valset, preferred_element_type=single)
    inner = jnp.sum(probs * prob_grad, axis=-1, keepdims=True)
    score_grad = (probs * (prob_grad - inner) * factor).astype(jnp.bfloat16)
    query_grad = jnp.einsum(
        "hqk,khd->qhd", score_grad, keyset, preferred_element_type=single
    ).reshape(length, width)
    key_grad = jnp.einsum("hqk,qhd->khd", score_grad, query, preferred_element_type=single).reshape(
        length, width
    )
    value_grad = jnp.einsum(
        "hqk,qhd->khd", probs_half, attended_grad, preferred_element_type=single
    ).reshape(length, width)
    packed_grad = jnp.concatenate([query_grad, key_grad, value_grad], axis=1).astype(jnp.bfloat16)
    grad_qkv = jnp.einsum("lc,lf->cf", hidden, packed_grad, preferred_element_type=single)
    grad_qbias = jnp.sum(packed_grad.astype(single), axis=0)
    hidden_grad = jnp.einsum("lf,cf->lc", packed_grad, qkv_weight, preferred_element_type=single)
    grad_gain = jnp.sum(hidden_grad * normed, axis=0)
    grad_nbias = jnp.sum(hidden_grad, axis=0)
    normed_grad = hidden_grad * norm_gain
    first = jnp.mean(normed_grad, axis=-1, keepdims=True)
    second = jnp.mean(normed_grad * normed, axis=-1, keepdims=True)
    token_grad = (upward.astype(single) + inverse * (normed_grad - first - normed * second)).astype(
        jnp.bfloat16
    )
    return (token_grad, (grad_qkv, grad_qbias, grad_proj, grad_pbias, grad_gain, grad_nbias))


def to_windows(block):
    sizes = block.shape[:3]
    rest = block.shape[3:]
    shaped = block.reshape(
        (sizes[0] // WIN, WIN, sizes[1] // WIN, WIN, sizes[2] // WIN, WIN) + rest
    )
    order = (0, 2, 4, 1, 3, 5) + tuple(range(6, 6 + len(rest)))
    return shaped.transpose(order).reshape((-1, WIN**3) + rest)


def from_windows(wins, first, second, third):
    rest = wins.shape[2:]
    shaped = wins.reshape((first // WIN, second // WIN, third // WIN, WIN, WIN, WIN) + rest)
    order = (0, 3, 1, 4, 2, 5) + tuple(range(6, 6 + len(rest)))
    return shaped.transpose(order).reshape((first, second, third) + rest)


def move_first(pieces):
    sent = passed_along((pieces[0][:SHIFT], pieces[1][:SHIFT]), "gx", -1)
    return (
        jnp.concatenate([pieces[0][SHIFT:], sent[0]], axis=0),
        jnp.concatenate([pieces[1][SHIFT:], sent[1]], axis=0),
    )


def move_second(pieces):
    sent = passed_along((pieces[0][:, :SHIFT], pieces[1][:, :SHIFT]), "gy", -1)
    return (
        jnp.concatenate([pieces[0][:, SHIFT:], sent[0]], axis=1),
        jnp.concatenate([pieces[1][:, SHIFT:], sent[1]], axis=1),
    )


def move_third(pieces):
    sent = passed_along((pieces[0][:, :, :SHIFT], pieces[1][:, :, :SHIFT]), "gz", -1)
    return (
        jnp.concatenate([pieces[0][:, :, SHIFT:], sent[0]], axis=2),
        jnp.concatenate([pieces[1][:, :, SHIFT:], sent[1]], axis=2),
    )


def window_index(count, position, length):
    total = length * count
    rolled = position * length + jnp.arange(length, dtype=jnp.int32)
    placed = (rolled + SHIFT) % total
    return ((placed + SHIFT) // WIN, total // WIN + 1, count)


def per_device(tokens, upstream, norm_gain, norm_bias, qkv_weight, qkv_bias, proj_weight):
    pieces = (tokens, upstream)
    pieces = move_third(move_second(move_first(pieces)))
    rolled, rolled_up = pieces
    depth_x, depth_y, depth_z, width = tokens.shape
    index_x, span_x, count_x = window_index(lax.axis_size("gx"), lax.axis_index("gx"), depth_x)
    index_y, span_y, count_y = window_index(lax.axis_size("gy"), lax.axis_index("gy"), depth_y)
    index_z, span_z, count_z = window_index(lax.axis_size("gz"), lax.axis_index("gz"), depth_z)
    idents = (index_x[:, None, None] * span_y + index_y[None, :, None]) * span_z + index_z[
        None, None, :
    ]
    token_wins = to_windows(rolled)
    up_wins = to_windows(rolled_up)
    ident_wins = to_windows(idents)
    zeros = (
        jnp.zeros((width, 3 * width), jnp.float32),
        jnp.zeros((3 * width,), jnp.float32),
        jnp.zeros((width, width), jnp.float32),
        jnp.zeros((width,), jnp.float32),
        jnp.zeros((width,), jnp.float32),
        jnp.zeros((width,), jnp.float32),
    )

    def advance(carry, item):
        grad_win, parts = window_grads(
            item[0], item[1], item[2], norm_gain, norm_bias, qkv_weight, qkv_bias, proj_weight
        )
        return (tuple((old + new for old, new in zip(carry, parts))), grad_win)

    totals, grad_wins = lax.scan(advance, zeros, (token_wins, up_wins, ident_wins))
    token_grad = from_windows(grad_wins, depth_x, depth_y, depth_z)
    summed = lax.psum(
        (totals[0], totals[1], totals[2], totals[3], totals[4], totals[5]), ("gx", "gy", "gz")
    )
    factor = float(depth_x * depth_y * depth_z * count_x * count_y * count_z) ** (-0.5)
    return (
        token_grad,
        summed[0] * factor,
        summed[1] * factor,
        summed[2] * factor,
        summed[3] * factor,
        summed[4] * factor,
        summed[5] * factor,
    )


def solution(mesh):
    placed = (P("gx", "gy", "gz", None), P("gx", "gy", "gz", None), P(), P(), P(), P(), P())
    return jax.shard_map(
        per_device,
        mesh=mesh,
        in_specs=placed,
        out_specs=(P("gx", "gy", "gz", None), P(), P(), P(), P(), P(), P()),
        check_vma=False,
    )
```

profile of v0, /device:TPU:6, one launch (start us, length us, event | category | flops | bytes accessed | tf_op | source)
XLA Modules:
  0.0 495.6 jit_solution(13295949907634760316)
XLA Ops:
  11.8 13.8 %collective-permute-done = bf16[4,16,16,192]{3,2,1,0:T(8,128)(2,1)S(1)} collective-permute-done((bf16[4,16,16,192]{3,2,1,0:T(8,128)(2,1)S(1)}, bf16[4,16,16,192]{3,2,1,0:T(8,128)(2,1)S(1)}, u32[]{:S(2)}, u32[]{:S(2)}) %collective-permute-start) | collective-permute-done | bytes 393248 | tf_op jit(solution)/shard_map/ppermute | solution.py:14
  25.7 9.9 %collective-permute-done.3 = bf16[4,16,16,192]{3,2,1,0:T(8,128)(2,1)S(1)} collective-permute-done((bf16[4,16,16,192]{3,2,1,0:T(8,128)(2,1)S(1)}, bf16[4,16,16,192]{3,2,1,0:T(8,128)(2,1)S(1)}, u32[]{:S(2)}, u32[]{:S(2)}) %collective-permute-start.3) | collective-permute-done | bytes 393248 | tf_op jit(solution)/shard_map/ppermute | solution.py:14
  36.1 9.7 %collective-permute-start.2 = (bf16[8,16,4,192]{3,2,1,0:T(4,128)(2,1)S(1)}, bf16[8,16,4,192]{3,2,1,0:T(4,128)(2,1)S(1)}, u32[]{:S(2)}, u32[]{:S(2)}) collective-permute-start(bf16[8,16,4,192]{3,2,1,0:T(4,128)(2,1)S(1)} %pad_maximum_fusion.7), channel_id=1, source_target_pairs={{0,7},{1,0},{2,1},{3,2},{4,3},{5,4},{6,5},{7,6},{8,15},{9,8},{10,9... | collective-permute-start | bytes 589832 | tf_op jit(solution)/shard_map/ppermute | solution.py:14
  48.4 5.1 %collective-permute-done.2 = bf16[8,16,4,192]{3,2,1,0:T(4,128)(2,1)S(1)} collective-permute-done((bf16[8,16,4,192]{3,2,1,0:T(4,128)(2,1)S(1)}, bf16[8,16,4,192]{3,2,1,0:T(4,128)(2,1)S(1)}, u32[]{:S(2)}, u32[]{:S(2)}) %collective-permute-start.2) | collective-permute-done | bytes 196640 | tf_op jit(solution)/shard_map/ppermute | solution.py:14
  54.9 14.1 %collective-permute-done.5 = bf16[8,16,4,192]{3,2,1,0:T(4,128)(2,1)} collective-permute-done((bf16[8,16,4,192]{3,2,1,0:T(4,128)(2,1)}, bf16[8,16,4,192]{3,2,1,0:T(4,128)(2,1)}, u32[]{:S(2)}, u32[]{:S(2)}) %collective-permute-start.5) | collective-permute-done | bytes 196640 | tf_op jit(solution)/shard_map/ppermute | solution.py:14
  71.2 158.2 %while.23 = (s32[]{:T(128)}, f32[192,576]{1,0:T(8,128)S(1)}, f32[576]{0:T(1024)S(1)}, f32[192,192]{1,0:T(8,128)S(1)}, f32[192]{0:T(256)S(1)}, /*index=5*/f32[192...) while((s32[]{:T(128)}, f32[192,576]{1,0:T(8,128)S(1)}, ...), condition=%wide.region_12.13_spmd.clone, body=%wide.region_0.12_spmd.clone.sunk | while | flops 1065100416 | bytes 87224056 | solution.py:154
  73.3 5.1 %fusion.146 = (f32[6,512]{1,0:T(8,128)S(1)}, f32[6,512,512]{1,2,0:T(8,128)}) fusion(pred[512,512]{0,1:T(8,128)(4,1)S(1)} %broadcast_compare_fusion.2, bf16[512,6,32]{0,2,1:T(8,128)(2,1)S(1)} %bitcast.162, bf16[512,6,32]{0,2,1:T(8,128)(2,1)S(1)} %bitcast.164), kind=kOutput, calls=%fused_computation.127.clone.1 | convolution fusion | flops 106955264 | bytes 6959104 | tf_op jit(solution)/shard_map/while/body/eval_jaxpr/sub | solution.py:39
  84.0 3.7 fusion.148
  87.7 10.8 %fusion.150 = bf16[6,32,512]{2,1,0:T(8,128)(2,1)S(1)} fusion(bf16[512,6,32]{0,2,1:T(8,128)(2,1)S(1)} %bitcast.165, f32[6,512,512]{1,2,0:T(8,128)} %fusion.148, f32[6,512,512]{1,2,0:T(8,128)} %get-tuple-element.353, f32[6,512]{1,0:T(8,128)S(1)} %get-tuple-element.354), kind=kOutput, calls=%fused_computation.22.clone.1 | convolution fusion | flops 111775232 | bytes 12988416 | tf_op jit(solution)/shard_map/while/body/eval_jaxpr/hqk,khd->qhd/dot_general | solution.py:53
  98.5 9.3 %fusion.149 = bf16[6,32,512]{2,1,0:T(8,128)(2,1)S(1)} fusion(bf16[512,6,32]{0,2,1:T(8,128)(2,1)S(1)} %bitcast.163, f32[6,512,512]{1,2,0:T(8,128)} %fusion.148, f32[6,512,512]{1,2,0:T(8,128)} %get-tuple-element.353, f32[6,512]{1,0:T(8,128)S(1)} %get-tuple-element.354), kind=kOutput, calls=%fused_computation.23.clone.1 | convolution fusion | flops 111775232 | bytes 12988416 | tf_op jit(solution)/shard_map/while/body/eval_jaxpr/hqk,qhd->khd/dot_general | solution.py:56
  112.8 5.1 %fusion.146 = (f32[6,512]{1,0:T(8,128)S(1)}, f32[6,512,512]{1,2,0:T(8,128)}) fusion(pred[512,512]{0,1:T(8,128)(4,1)S(1)} %broadcast_compare_fusion.2, bf16[512,6,32]{0,2,1:T(8,128)(2,1)S(1)} %bitcast.162, bf16[512,6,32]{0,2,1:T(8,128)(2,1)S(1)} %bitcast.164), kind=kOutput, calls=%fused_computation.127.clone.1 | convolution fusion | flops 106955264 | bytes 6959104 | tf_op jit(solution)/shard_map/while/body/eval_jaxpr/sub | solution.py:39
  123.6 3.7 fusion.148
  127.3 10.8 %fusion.150 = bf16[6,32,512]{2,1,0:T(8,128)(2,1)S(1)} fusion(bf16[512,6,32]{0,2,1:T(8,128)(2,1)S(1)} %bitcast.165, f32[6,512,512]{1,2,0:T(8,128)} %fusion.148, f32[6,512,512]{1,2,0:T(8,128)} %get-tuple-element.353, f32[6,512]{1,0:T(8,128)S(1)} %get-tuple-element.354), kind=kOutput, calls=%fused_computation.22.clone.1 | convolution fusion | flops 111775232 | bytes 12988416 | tf_op jit(solution)/shard_map/while/body/eval_jaxpr/hqk,khd->qhd/dot_general | solution.py:53
  138.1 9.3 %fusion.149 = bf16[6,32,512]{2,1,0:T(8,128)(2,1)S(1)} fusion(bf16[512,6,32]{0,2,1:T(8,128)(2,1)S(1)} %bitcast.163, f32[6,512,512]{1,2,0:T(8,128)} %fusion.148, f32[6,512,512]{1,2,0:T(8,128)} %get-tuple-element.353, f32[6,512]{1,0:T(8,128)S(1)} %get-tuple-element.354), kind=kOutput, calls=%fused_computation.23.clone.1 | convolution fusion | flops 111775232 | bytes 12988416 | tf_op jit(solution)/shard_map/while/body/eval_jaxpr/hqk,qhd->khd/dot_general | solution.py:56
  152.4 5.1 %fusion.146 = (f32[6,512]{1,0:T(8,128)S(1)}, f32[6,512,512]{1,2,0:T(8,128)}) fusion(pred[512,512]{0,1:T(8,128)(4,1)S(1)} %broadcast_compare_fusion.2, bf16[512,6,32]{0,2,1:T(8,128)(2,1)S(1)} %bitcast.162, bf16[512,6,32]{0,2,1:T(8,128)(2,1)S(1)} %bitcast.164), kind=kOutput, calls=%fused_computation.127.clone.1 | convolution fusion | flops 106955264 | bytes 6959104 | tf_op jit(solution)/shard_map/while/body/eval_jaxpr/sub | solution.py:39
  163.1 3.7 fusion.148
  166.8 10.8 %fusion.150 = bf16[6,32,512]{2,1,0:T(8,128)(2,1)S(1)} fusion(bf16[512,6,32]{0,2,1:T(8,128)(2,1)S(1)} %bitcast.165, f32[6,512,512]{1,2,0:T(8,128)} %fusion.148, f32[6,512,512]{1,2,0:T(8,128)} %get-tuple-element.353, f32[6,512]{1,0:T(8,128)S(1)} %get-tuple-element.354), kind=kOutput, calls=%fused_computation.22.clone.1 | convolution fusion | flops 111775232 | bytes 12988416 | tf_op jit(solution)/shard_map/while/body/eval_jaxpr/hqk,khd->qhd/dot_general | solution.py:53
  177.6 9.3 %fusion.149 = bf16[6,32,512]{2,1,0:T(8,128)(2,1)S(1)} fusion(bf16[512,6,32]{0,2,1:T(8,128)(2,1)S(1)} %bitcast.163, f32[6,512,512]{1,2,0:T(8,128)} %fusion.148, f32[6,512,512]{1,2,0:T(8,128)} %get-tuple-element.353, f32[6,512]{1,0:T(8,128)S(1)} %get-tuple-element.354), kind=kOutput, calls=%fused_computation.23.clone.1 | convolution fusion | flops 111775232 | bytes 12988416 | tf_op jit(solution)/shard_map/while/body/eval_jaxpr/hqk,qhd->khd/dot_general | solution.py:56
  191.9 5.1 %fusion.146 = (f32[6,512]{1,0:T(8,128)S(1)}, f32[6,512,512]{1,2,0:T(8,128)}) fusion(pred[512,512]{0,1:T(8,128)(4,1)S(1)} %broadcast_compare_fusion.2, bf16[512,6,32]{0,2,1:T(8,128)(2,1)S(1)} %bitcast.162, bf16[512,6,32]{0,2,1:T(8,128)(2,1)S(1)} %bitcast.164), kind=kOutput, calls=%fused_computation.127.clone.1 | convolution fusion | flops 106955264 | bytes 6959104 | tf_op jit(solution)/shard_map/while/body/eval_jaxpr/sub | solution.py:39
  202.7 3.7 fusion.148
  206.4 10.8 %fusion.150 = bf16[6,32,512]{2,1,0:T(8,128)(2,1)S(1)} fusion(bf16[512,6,32]{0,2,1:T(8,128)(2,1)S(1)} %bitcast.165, f32[6,512,512]{1,2,0:T(8,128)} %fusion.148, f32[6,512,512]{1,2,0:T(8,128)} %get-tuple-element.353, f32[6,512]{1,0:T(8,128)S(1)} %get-tuple-element.354), kind=kOutput, calls=%fused_computation.22.clone.1 | convolution fusion | flops 111775232 | bytes 12988416 | tf_op jit(solution)/shard_map/while/body/eval_jaxpr/hqk,khd->qhd/dot_general | solution.py:53
  217.2 9.3 %fusion.149 = bf16[6,32,512]{2,1,0:T(8,128)(2,1)S(1)} fusion(bf16[512,6,32]{0,2,1:T(8,128)(2,1)S(1)} %bitcast.163, f32[6,512,512]{1,2,0:T(8,128)} %fusion.148, f32[6,512,512]{1,2,0:T(8,128)} %get-tuple-element.353, f32[6,512]{1,0:T(8,128)S(1)} %get-tuple-element.354), kind=kOutput, calls=%fused_computation.23.clone.1 | convolution fusion | flops 111775232 | bytes 12988416 | tf_op jit(solution)/shard_map/while/body/eval_jaxpr/hqk,qhd->khd/dot_general | solution.py:56
  230.3 76.7 %all-reduce = (f32[576]{0:T(1024)S(1)}, f32[192]{0:T(256)S(1)}, f32[192]{0:T(256)S(1)}, f32[192]{0:T(256)S(1)}) all-reduce(f32[576]{0:T(1024)S(1)} %get-tuple-element.97, f32[192]{0:T(256)S(1)} %get-tuple-element.99, f32[192]{0:T(256)S(1)} %get-tuple-element.100, ...), channel_id=1, replica_groups=mesh['gx'=16,'gy'=2,'gz'=8] {'gx','gy','gz'}, use_global_device_ids=true, to_apply=%region_14.15 | all-reduce | flops 1152 | bytes 9216 | tf_op jit(solution)/shard_map/psum | solution.py:156
  311.2 174.0 %all-reduce.4.cloned.1.call-done = (f32[192,576]{1,0:T(8,128)}, f32[192,192]{1,0:T(8,128)}) async-done(((f32[192,576]{1,0:T(8,128)}, f32[192,192]{1,0:T(8,128)}), (f32[192,576]{1,0:T(8,128)}, f32[192,192]{1,0:T(8,128)})) %all-reduce.4.cloned.1.call-update) | async-done | bytes 589840 | tf_op jit(solution)/shard_map/psum | solution.py:156
  (155 shorter events, 62.1 us)
Async XLA Ops:
  7.2 478.1 %all-reduce.4.cloned.1.call-start = ((), (), s32[]{:S(2)}) async-start(), calls=%async_computation | async-start | bytes 1376256 | tf_op jit(solution)/shard_map/psum | solution.py:156
  8.5 17.0 %collective-permute-start = (bf16[4,16,16,192]{3,2,1,0:T(8,128)(2,1)S(1)}, bf16[4,16,16,192]{3,2,1,0:T(8,128)(2,1)S(1)}, u32[]{:S(2)}, u32[]{:S(2)}) collective-permute-start(bf16[4,16,16,192]{3,2,1,0:T(8,128)(2,1)S(1)} %get-tuple-element.238), channel_id=1, source_target_pairs={{0,240},{16,0},{32,16},{48,32},{64,48},{80,64},{96,80},{112,96},{1... | collective-permute-start | bytes 1179656 | tf_op jit(solution)/shard_map/ppermute | solution.py:14
  10.7 24.9 %collective-permute-start.3 = (bf16[4,16,16,192]{3,2,1,0:T(8,128)(2,1)S(1)}, bf16[4,16,16,192]{3,2,1,0:T(8,128)(2,1)S(1)}, u32[]{:S(2)}, u32[]{:S(2)}) collective-permute-start(bf16[4,16,16,192]{3,2,1,0:T(8,128)(2,1)S(1)} %get-tuple-element.236), channel_id=1, source_target_pairs={{0,240},{16,0},{32,16},{48,32},{64,48},{80,64},{96,80},{112,96},{1... | collective-permute-start | bytes 1179656 | tf_op jit(solution)/shard_map/ppermute | solution.py:14
  25.6 10.5 %collective-permute-start.1 = (bf16[8,4,16,192]{3,2,1,0:T(8,128)(2,1)S(1)}, bf16[8,4,16,192]{3,2,1,0:T(8,128)(2,1)S(1)}, u32[]{:S(2)}, u32[]{:S(2)}) collective-permute-start(bf16[8,4,16,192]{3,2,1,0:T(8,128)(2,1)S(1)} %pad_maximum_fusion.8), channel_id=1, source_target_pairs={{0,8},{8,0},{1,9},{9,1},{2,10},{10,2},{3,11},{11,3},{4,12},{12,4},... | collective-permute-start | bytes 589832 | tf_op jit(solution)/shard_map/ppermute | solution.py:14
  35.7 10.2 %collective-permute-start.4 = (bf16[8,4,16,192]{3,2,1,0:T(8,128)(2,1)S(1)}, bf16[8,4,16,192]{3,2,1,0:T(8,128)(2,1)S(1)}, u32[]{:S(2)}, u32[]{:S(2)}) collective-permute-start(bf16[8,4,16,192]{3,2,1,0:T(8,128)(2,1)S(1)} %pad_maximum_fusion.6), channel_id=1, source_target_pairs={{0,8},{8,0},{1,9},{9,1},{2,10},{10,2},{3,11},{11,3},{4,12},{12,4},... | collective-permute-start | bytes 589832 | tf_op jit(solution)/shard_map/ppermute | solution.py:14
  36.1 17.4 %collective-permute-start.2 = (bf16[8,16,4,192]{3,2,1,0:T(4,128)(2,1)S(1)}, bf16[8,16,4,192]{3,2,1,0:T(4,128)(2,1)S(1)}, u32[]{:S(2)}, u32[]{:S(2)}) collective-permute-start(bf16[8,16,4,192]{3,2,1,0:T(4,128)(2,1)S(1)} %pad_maximum_fusion.7), channel_id=1, source_target_pairs={{0,7},{1,0},{2,1},{3,2},{4,3},{5,4},{6,5},{7,6},{8,15},{9,8},{10,9... | collective-permute-start | bytes 589832 | tf_op jit(solution)/shard_map/ppermute | solution.py:14
  46.6 22.4 %collective-permute-start.5 = (bf16[8,16,4,192]{3,2,1,0:T(4,128)(2,1)}, bf16[8,16,4,192]{3,2,1,0:T(4,128)(2,1)}, u32[]{:S(2)}, u32[]{:S(2)}) collective-permute-start(bf16[8,16,4,192]{3,2,1,0:T(4,128)(2,1)} %pad_maximum_fusion.5), channel_id=1, source_target_pairs={{0,7},{1,0},{2,1},{3,2},{4,3},{5,4},{6,5},{7,6},{8,15},{9,8},{10,9... | collective-permute-start | bytes 589832 | tf_op jit(solution)/shard_map/ppermute | solution.py:14
  48.3 22.8 %copy-start.1 = (bf16[192,192]{1,0:T(8,128)(2,1)S(1)}, bf16[192,192]{1,0:T(8,128)(2,1)}, u32[]{:S(2)}) copy-start(bf16[192,192]{1,0:T(8,128)(2,1)} %param.15) | copy-start | bytes 221188
  48.3 22.8 %copy-start.4 = (f32[192]{0:T(256)S(1)}, f32[192]{0:T(256)}, u32[]{:S(2)}) copy-start(f32[192]{0:T(256)} %param.11) | copy-start | bytes 2308
  48.4 22.8 %copy-start.5 = (f32[576]{0:T(1024)S(1)}, f32[576]{0:T(1024)}, u32[]{:S(2)}) copy-start(f32[576]{0:T(1024)} %param.14) | copy-start | bytes 6916
  48.4 22.8 %copy-start.6 = (f32[192]{0:T(256)S(1)}, f32[192]{0:T(256)}, u32[]{:S(2)}) copy-start(f32[192]{0:T(256)} %param.12) | copy-start | bytes 2308
  54.9 16.3 %copy-start.2 = (f32[192,576]{1,0:T(8,128)S(1)}, f32[192,576]{1,0:T(8,128)}, u32[]{:S(2)}) copy-start(f32[192,576]{1,0:T(8,128)} %custom-call) | copy-start | bytes 1327108
  78.4 4.6 copy-start.7
  117.9 4.6 copy-start.7
  157.5 4.6 copy-start.7
  197.0 4.6 copy-start.7
  229.4 0.7 copy-start
  229.4 0.8 copy-start.3
Sparse Core Ops, SparseCore 0:
  230.4 254.8 all-reduce.3
where the time goes:
time: 496 us
  waiting for transfers between devices  217 us (44%)
  matrix products  149 us (30%)
  blocking collectives  76.7 us (15%)
  other arithmetic  15.2 us (3%)
  between operations  14.3 us (3%)
  starting transfers between devices  12.5 us (3%)
  local copies, waits for them, and re-layouts  10.6 us (2%)
    psum x1, waiting for transfers between devices, per_device(): lax.psum((totals[0], totals[1], totals[2], totals[3], totals[4], totals[5...  174 us
    psum x1, blocking collectives, per_device(): lax.psum((totals[0], totals[1], totals[2], totals[3], totals[4], totals[5...  76.7 us
    dot_general x4, matrix products, window_grads(): jnp.einsum('hqk,khd->qhd', score_grad, keyset, preferred_element_type=sin...  43.1 us
    ppermute x6, waiting for transfers between devices, passed_along(): return lax.ppermute(value, axis, pairs)  42.9 us
    dot_general x4, matrix products, window_grads(): jnp.einsum('hqk,qhd->khd', score_grad, query, preferred_element_type=single)  37 us
    sub x4, matrix products, window_grads(): expo = jnp.exp(scores - peak)  20.4 us
    dot_general x4, matrix products, window_grads(): jnp.einsum('qhd,khd->hqk', attended_grad, valset, preferred_element_type=...  14.8 us
    dot_general x4, matrix products, window_grads(): jnp.einsum('hqk,khd->qhd', probs_half, valset, preferred_element_type=sin...  14.3 us
  transfers between devices with their start and end apart: 7, of which 5 were waited for; matrix products, arithmetic and copies ran while one was open for 2% of the time, Pallas kernels for 0%

commit v1 on v0

--- a/solution.py
+++ b/solution.py
@@ -6,6 +6,11 @@
 HEADS = 6
 WIN = 8
 SHIFT = 4
+
+
+def by_each_axis(value_2, one, other):
+    half = lax.psum(value_2, one)
+    return lax.psum(half, other)
 
 
 def passed_along(value, axis, steps):
@@ -153,8 +158,8 @@
 
     totals, grad_wins = lax.scan(advance, zeros, (token_wins, up_wins, ident_wins))
     token_grad = from_windows(grad_wins, depth_x, depth_y, depth_z)
-    summed = lax.psum(
-        (totals[0], totals[1], totals[2], totals[3], totals[4], totals[5]), ("gx", "gy", "gz")
+    summed = by_each_axis(
+        (totals[0], totals[1], totals[2], totals[3], totals[4], totals[5]), ("gy", "gz"), "gx"
     )
     factor = float(depth_x * depth_y * depth_z * count_x * count_y * count_z) ** (-0.5)
     return (

time: 496 us -> 599 us (1.21)
  waiting for transfers between devices: 217 us -> 302 us
  blocking collectives: 76.7 us -> 83.5 us
  matrix products: 149 us -> 155 us
    psum x1 -> x2, waiting for transfers between devices: 174 us -> 258 us  [the longest x1 157 us: by_each_axis(): return lax.psum(half, other)]
    psum x1 -> x2, blocking collectives: 76.7 us -> 83.5 us  [the longest x1 51.8 us: by_each_axis(): half = lax.psum(value_2, one)]
    dot_general x4, matrix products: 1.69 us -> 7.82 us  [window_grads(): jnp.einsum('lc,lf->cf', hidden, packed_grad, preferred_element_type=single)]
  transfers between devices with their start and end apart: 7 -> 8, of which waited for: 5 -> 6; matrix products, arithmetic and copies ran while one was open for 2% -> 2% of each run, Pallas kernels for 0% -> 0%
where the time goes in v1:
time: 599 us; the launch traced here: 594 us
  waiting for transfers between devices  302 us (50%)
  matrix products  155 us (26%)
  blocking collectives  83.5 us (14%)
  other arithmetic  15.1 us (3%)
  between operations  14.3 us (2%)
  starting transfers between devices  12.5 us (2%)
  local copies, waits for them, and re-layouts  11.3 us (2%)
    psum x1, waiting for transfers between devices, by_each_axis(): return lax.psum(half, other)  157 us
    psum x1, waiting for transfers between devices, by_each_axis(): half = lax.psum(value_2, one)  101 us
    psum x1, blocking collectives, by_each_axis(): half = lax.psum(value_2, one)  51.8 us
    ppermute x6, waiting for transfers between devices, passed_along(): return lax.ppermute(value, axis, pairs)  43.2 us
    dot_general x4, matrix products, window_grads(): jnp.einsum('hqk,khd->qhd', score_grad, keyset, preferred_element_type=sin...  43.1 us
    dot_general x4, matrix products, window_grads(): jnp.einsum('hqk,qhd->khd', score_grad, query, preferred_element_type=single)  37.1 us
    psum x1, blocking collectives, by_each_axis(): return lax.psum(half, other)  31.7 us
    sub x4, matrix products, window_grads(): expo = jnp.exp(scores - peak)  20.4 us
  transfers between devices with their start and end apart: 8, of which 6 were waited for; matrix products, arithmetic and copies ran while one was open for 2% of the time, Pallas kernels for 0%

profile of v1, /device:TPU:6, one launch (start us, length us, event | category | flops | bytes accessed | tf_op | source)
XLA Modules:
  0.0 593.5 jit_solution(16049172843050234554)
XLA Ops:
  12.5 14.0 %collective-permute-done = bf16[4,16,16,192]{3,2,1,0:T(8,128)(2,1)S(1)} collective-permute-done((bf16[4,16,16,192]{3,2,1,0:T(8,128)(2,1)}, bf16[4,16,16,192]{3,2,1,0:T(8,128)(2,1)S(1)}, u32[]{:S(2)}, u32[]{:S(2)}) %collective-permute-start) | collective-permute-done | bytes 393248 | tf_op jit(solution)/shard_map/ppermute | solution.py:19
  26.6 9.9 %collective-permute-done.3 = bf16[4,16,16,192]{3,2,1,0:T(8,128)(2,1)S(1)} collective-permute-done((bf16[4,16,16,192]{3,2,1,0:T(8,128)(2,1)S(1)}, bf16[4,16,16,192]{3,2,1,0:T(8,128)(2,1)S(1)}, u32[]{:S(2)}, u32[]{:S(2)}) %collective-permute-start.3) | collective-permute-done | bytes 393248 | tf_op jit(solution)/shard_map/ppermute | solution.py:19
  37.1 9.7 %collective-permute-start.2 = (bf16[8,16,4,192]{3,2,1,0:T(4,128)(2,1)S(1)}, bf16[8,16,4,192]{3,2,1,0:T(4,128)(2,1)S(1)}, u32[]{:S(2)}, u32[]{:S(2)}) collective-permute-start(bf16[8,16,4,192]{3,2,1,0:T(4,128)(2,1)S(1)} %pad_maximum_fusion.7), channel_id=1, source_target_pairs={{0,7},{1,0},{2,1},{3,2},{4,3},{5,4},{6,5},{7,6},{8,15},{9,8},{10,9... | collective-permute-start | bytes 589832 | tf_op jit(solution)/shard_map/ppermute | solution.py:19
  49.3 5.1 collective-permute-done.2
  55.8 14.1 %collective-permute-done.5 = bf16[8,16,4,192]{3,2,1,0:T(4,128)(2,1)} collective-permute-done((bf16[8,16,4,192]{3,2,1,0:T(4,128)(2,1)}, bf16[8,16,4,192]{3,2,1,0:T(4,128)(2,1)}, u32[]{:S(2)}, u32[]{:S(2)}) %collective-permute-start.5) | collective-permute-done | bytes 196640 | tf_op jit(solution)/shard_map/ppermute | solution.py:19
  72.1 164.3 %while.23 = (s32[]{:T(128)}, f32[192,576]{1,0:T(8,128)}, f32[576]{0:T(1024)S(1)}, f32[192,192]{1,0:T(8,128)S(1)}, f32[192]{0:T(256)S(1)}, /*index=5*/f32[192]{0:...) while((s32[]{:T(128)}, f32[192,576]{1,0:T(8,128)}, ...), condition=%wide.region_12.13_spmd.clone, body=%wide.region_0.12_spmd.clone.sunk | while | flops 1065100416 | bytes 87174904 | solution.py:159
  74.2 5.1 fusion.146
  84.9 3.7 fusion.148
  88.6 10.8 %fusion.150 = bf16[6,32,512]{2,1,0:T(8,128)(2,1)S(1)} fusion(bf16[512,6,32]{0,2,1:T(8,128)(2,1)S(1)} %bitcast.165, f32[6,512,512]{1,2,0:T(8,128)} %fusion.148, f32[6,512,512]{1,2,0:T(8,128)} %get-tuple-element.359, f32[6,512]{1,0:T(8,128)S(1)} %get-tuple-element.360), kind=kOutput, calls=%fused_computation.22.clone.1 | convolution fusion | flops 111775232 | bytes 12988416 | tf_op jit(solution)/shard_map/while/body/eval_jaxpr/hqk,khd->qhd/dot_general | solution.py:58
  99.4 9.3 %fusion.149 = bf16[6,32,512]{2,1,0:T(8,128)(2,1)S(1)} fusion(bf16[512,6,32]{0,2,1:T(8,128)(2,1)S(1)} %bitcast.163, f32[6,512,512]{1,2,0:T(8,128)} %fusion.148, f32[6,512,512]{1,2,0:T(8,128)} %get-tuple-element.359, f32[6,512]{1,0:T(8,128)S(1)} %get-tuple-element.360), kind=kOutput, calls=%fused_computation.23.clone.1 | convolution fusion | flops 111775232 | bytes 12988416 | tf_op jit(solution)/shard_map/while/body/eval_jaxpr/hqk,qhd->khd/dot_general | solution.py:61
  114.5 5.1 fusion.146
  125.2 3.7 fusion.148
  128.9 10.8 %fusion.150 = bf16[6,32,512]{2,1,0:T(8,128)(2,1)S(1)} fusion(bf16[512,6,32]{0,2,1:T(8,128)(2,1)S(1)} %bitcast.165, f32[6,512,512]{1,2,0:T(8,128)} %fusion.148, f32[6,512,512]{1,2,0:T(8,128)} %get-tuple-element.359, f32[6,512]{1,0:T(8,128)S(1)} %get-tuple-element.360), kind=kOutput, calls=%fused_computation.22.clone.1 | convolution fusion | flops 111775232 | bytes 12988416 | tf_op jit(solution)/shard_map/while/body/eval_jaxpr/hqk,khd->qhd/dot_general | solution.py:58
  139.7 9.3 %fusion.149 = bf16[6,32,512]{2,1,0:T(8,128)(2,1)S(1)} fusion(bf16[512,6,32]{0,2,1:T(8,128)(2,1)S(1)} %bitcast.163, f32[6,512,512]{1,2,0:T(8,128)} %fusion.148, f32[6,512,512]{1,2,0:T(8,128)} %get-tuple-element.359, f32[6,512]{1,0:T(8,128)S(1)} %get-tuple-element.360), kind=kOutput, calls=%fused_computation.23.clone.1 | convolution fusion | flops 111775232 | bytes 12988416 | tf_op jit(solution)/shard_map/while/body/eval_jaxpr/hqk,qhd->khd/dot_general | solution.py:61
  155.8 5.1 fusion.146
  170.3 10.8 %fusion.150 = bf16[6,32,512]{2,1,0:T(8,128)(2,1)S(1)} fusion(bf16[512,6,32]{0,2,1:T(8,128)(2,1)S(1)} %bitcast.165, f32[6,512,512]{1,2,0:T(8,128)} %fusion.148, f32[6,512,512]{1,2,0:T(8,128)} %get-tuple-element.359, f32[6,512]{1,0:T(8,128)S(1)} %get-tuple-element.360), kind=kOutput, calls=%fused_computation.22.clone.1 | convolution fusion | flops 111775232 | bytes 12988416 | tf_op jit(solution)/shard_map/while/body/eval_jaxpr/hqk,khd->qhd/dot_general | solution.py:58
  181.1 9.3 %fusion.149 = bf16[6,32,512]{2,1,0:T(8,128)(2,1)S(1)} fusion(bf16[512,6,32]{0,2,1:T(8,128)(2,1)S(1)} %bitcast.163, f32[6,512,512]{1,2,0:T(8,128)} %fusion.148, f32[6,512,512]{1,2,0:T(8,128)} %get-tuple-element.359, f32[6,512]{1,0:T(8,128)S(1)} %get-tuple-element.360), kind=kOutput, calls=%fused_computation.23.clone.1 | convolution fusion | flops 111775232 | bytes 12988416 | tf_op jit(solution)/shard_map/while/body/eval_jaxpr/hqk,qhd->khd/dot_general | solution.py:61
  197.1 5.1 fusion.146
  211.6 10.8 %fusion.150 = bf16[6,32,512]{2,1,0:T(8,128)(2,1)S(1)} fusion(bf16[512,6,32]{0,2,1:T(8,128)(2,1)S(1)} %bitcast.165, f32[6,512,512]{1,2,0:T(8,128)} %fusion.148, f32[6,512,512]{1,2,0:T(8,128)} %get-tuple-element.359, f32[6,512]{1,0:T(8,128)S(1)} %get-tuple-element.360), kind=kOutput, calls=%fused_computation.22.clone.1 | convolution fusion | flops 111775232 | bytes 12988416 | tf_op jit(solution)/shard_map/while/body/eval_jaxpr/hqk,khd->qhd/dot_general | solution.py:58
  222.4 9.3 %fusion.149 = bf16[6,32,512]{2,1,0:T(8,128)(2,1)S(1)} fusion(bf16[512,6,32]{0,2,1:T(8,128)(2,1)S(1)} %bitcast.163, f32[6,512,512]{1,2,0:T(8,128)} %fusion.148, f32[6,512,512]{1,2,0:T(8,128)} %get-tuple-element.359, f32[6,512]{1,0:T(8,128)S(1)} %get-tuple-element.360), kind=kOutput, calls=%fused_computation.23.clone.1 | convolution fusion | flops 111775232 | bytes 12988416 | tf_op jit(solution)/shard_map/while/body/eval_jaxpr/hqk,qhd->khd/dot_general | solution.py:61
  239.6 51.8 %all-reduce = (f32[576]{0:T(1024)S(1)}, f32[192]{0:T(256)S(1)}, f32[192]{0:T(256)S(1)}, f32[192]{0:T(256)S(1)}) all-reduce(f32[576]{0:T(1024)S(1)} %get-tuple-element.97, f32[192]{0:T(256)S(1)} %get-tuple-element.99, f32[192]{0:T(256)S(1)} %get-tuple-element.100, ...), channel_id=1, replica_groups=mesh['gx'=16,'gy'=2,'gz'=8] {'gy','gz'}, use_global_device_ids=true, to_apply=%region_15.16 | all-reduce | flops 1152 | bytes 9216 | tf_op jit(solution)/shard_map/psum | solution.py:12
  291.4 31.7 %all-reduce.2 = (f32[576]{0:T(1024)S(1)}, f32[192]{0:T(256)S(1)}, f32[192]{0:T(256)S(1)}, f32[192]{0:T(256)S(1)}) all-reduce(f32[576]{0:T(1024)S(1)} %get-tuple-element.221, f32[192]{0:T(256)S(1)} %get-tuple-element.222, f32[192]{0:T(256)S(1)} %get-tuple-element.223, ...), channel_id=1, replica_groups=mesh['gx'=16,'gy'=2,'gz'=8] {'gx'}, use_global_device_ids=true, to_apply=%region_16.17 | all-reduce | flops 1152 | bytes 9216 | tf_op jit(solution)/shard_map/psum | solution.py:13
  323.2 100.8 %all-reduce.7.cloned.1.call-done = (f32[192,576]{1,0:T(8,128)}, f32[192,192]{1,0:T(8,128)}) async-done(((f32[192,576]{1,0:T(8,128)}, f32[192,192]{1,0:T(8,128)}), (f32[192,576]{1,0:T(8,128)}, f32[192,192]{1,0:T(8,128)})) %all-reduce.7.cloned.1.call-update) | async-done | bytes 589840 | tf_op jit(solution)/shard_map/psum | solution.py:12
  425.7 157.5 %all-reduce.9.cloned.1.call-done = (f32[192,576]{1,0:T(8,128)}, f32[192,192]{1,0:T(8,128)}) async-done(((f32[192,576]{1,0:T(8,128)}, f32[192,192]{1,0:T(8,128)}), (f32[192,576]{1,0:T(8,128)}, f32[192,192]{1,0:T(8,128)})) %all-reduce.9.cloned.1.call-update) | async-done | bytes 589840 | tf_op jit(solution)/shard_map/psum | solution.py:13
  (155 shorter events, 76.2 us)
Async XLA Ops:
  7.2 416.8 %all-reduce.7.cloned.1.call-start = ((), (), s32[]{:S(2)}) async-start(), calls=%async_computation | async-start | bytes 1376256 | tf_op jit(solution)/shard_map/psum | solution.py:12
  9.3 17.1 %collective-permute-start = (bf16[4,16,16,192]{3,2,1,0:T(8,128)(2,1)}, bf16[4,16,16,192]{3,2,1,0:T(8,128)(2,1)S(1)}, u32[]{:S(2)}, u32[]{:S(2)}) collective-permute-start(bf16[4,16,16,192]{3,2,1,0:T(8,128)(2,1)} %get-tuple-element.244), channel_id=1, source_target_pairs={{0,240},{16,0},{32,16},{48,32},{64,48},{80,64},{96,80},{112,96},{1... | collective-permute-start | bytes 1179656 | tf_op jit(solution)/shard_map/ppermute | solution.py:19
  11.4 25.1 %collective-permute-start.3 = (bf16[4,16,16,192]{3,2,1,0:T(8,128)(2,1)S(1)}, bf16[4,16,16,192]{3,2,1,0:T(8,128)(2,1)S(1)}, u32[]{:S(2)}, u32[]{:S(2)}) collective-permute-start(bf16[4,16,16,192]{3,2,1,0:T(8,128)(2,1)S(1)} %get-tuple-element.242), channel_id=1, source_target_pairs={{0,240},{16,0},{32,16},{48,32},{64,48},{80,64},{96,80},{112,96},{1... | collective-permute-start | bytes 1179656 | tf_op jit(solution)/shard_map/ppermute | solution.py:19
  26.5 10.5 %collective-permute-start.1 = (bf16[8,4,16,192]{3,2,1,0:T(8,128)(2,1)S(1)}, bf16[8,4,16,192]{3,2,1,0:T(8,128)(2,1)S(1)}, u32[]{:S(2)}, u32[]{:S(2)}) collective-permute-start(bf16[8,4,16,192]{3,2,1,0:T(8,128)(2,1)S(1)} %pad_maximum_fusion.8), channel_id=1, source_target_pairs={{0,8},{8,0},{1,9},{9,1},{2,10},{10,2},{3,11},{11,3},{4,12},{12,4},... | collective-permute-start | bytes 589832 | tf_op jit(solution)/shard_map/ppermute | solution.py:19
  36.6 10.2 %collective-permute-start.4 = (bf16[8,4,16,192]{3,2,1,0:T(8,128)(2,1)S(1)}, bf16[8,4,16,192]{3,2,1,0:T(8,128)(2,1)S(1)}, u32[]{:S(2)}, u32[]{:S(2)}) collective-permute-start(bf16[8,4,16,192]{3,2,1,0:T(8,128)(2,1)S(1)} %pad_maximum_fusion.6), channel_id=1, source_target_pairs={{0,8},{8,0},{1,9},{9,1},{2,10},{10,2},{3,11},{11,3},{4,12},{12,4},... | collective-permute-start | bytes 589832 | tf_op jit(solution)/shard_map/ppermute | solution.py:19
  37.1 17.4 %collective-permute-start.2 = (bf16[8,16,4,192]{3,2,1,0:T(4,128)(2,1)S(1)}, bf16[8,16,4,192]{3,2,1,0:T(4,128)(2,1)S(1)}, u32[]{:S(2)}, u32[]{:S(2)}) collective-permute-start(bf16[8,16,4,192]{3,2,1,0:T(4,128)(2,1)S(1)} %pad_maximum_fusion.7), channel_id=1, source_target_pairs={{0,7},{1,0},{2,1},{3,2},{4,3},{5,4},{6,5},{7,6},{8,15},{9,8},{10,9... | collective-permute-start | bytes 589832 | tf_op jit(solution)/shard_map/ppermute | solution.py:19
  47.6 22.4 %collective-permute-start.5 = (bf16[8,16,4,192]{3,2,1,0:T(4,128)(2,1)}, bf16[8,16,4,192]{3,2,1,0:T(4,128)(2,1)}, u32[]{:S(2)}, u32[]{:S(2)}) collective-permute-start(bf16[8,16,4,192]{3,2,1,0:T(4,128)(2,1)} %pad_maximum_fusion.5), channel_id=1, source_target_pairs={{0,7},{1,0},{2,1},{3,2},{4,3},{5,4},{6,5},{7,6},{8,15},{9,8},{10,9... | collective-permute-start | bytes 589832 | tf_op jit(solution)/shard_map/ppermute | solution.py:19
  49.2 22.8 %copy-start.1 = (bf16[192,192]{1,0:T(8,128)(2,1)S(1)}, bf16[192,192]{1,0:T(8,128)(2,1)}, u32[]{:S(2)}) copy-start(bf16[192,192]{1,0:T(8,128)(2,1)} %param.15) | copy-start | bytes 221188
  49.3 22.8 %copy-start.2 = (f32[192]{0:T(256)S(1)}, f32[192]{0:T(256)}, u32[]{:S(2)}) copy-start(f32[192]{0:T(256)} %param.11) | copy-start | bytes 2308
  49.3 22.8 %copy-start.3 = (f32[576]{0:T(1024)S(1)}, f32[576]{0:T(1024)}, u32[]{:S(2)}) copy-start(f32[576]{0:T(1024)} %param.14) | copy-start | bytes 6916
  49.3 22.8 %copy-start.4 = (f32[192]{0:T(256)S(1)}, f32[192]{0:T(256)}, u32[]{:S(2)}) copy-start(f32[192]{0:T(256)} %param.12) | copy-start | bytes 2308
  79.3 4.6 copy-start.5
  119.6 4.6 copy-start.5
  160.9 4.6 copy-start.5
  202.2 4.6 copy-start.5
  236.4 0.7 copy-start
  237.1 346.1 %all-reduce.9.cloned.1.call-start = ((), (), s32[]{:S(2)}) async-start(), calls=%async_computation.1 | async-start | bytes 1376256 | tf_op jit(solution)/shard_map/psum | solution.py:13
Sparse Core Ops, SparseCore 0:
  237.2 186.7 all-reduce.6
  426.9 156.2 all-reduce.8
